TPU v7x, 256 devices: a whole 4x4x8 slice. The times are simulated.
256 devices in a mesh: col: 4 (over z_lo, core), dp: 64 (over y, x, z_hi).
Axes of the slice: x: 4, y: 4, z: 8 (z_hi: 4, z_lo: 2; z = z_hi * 2 + z_lo), core: 2. Of those that a mesh axis runs over, the one named last changes fastest.
Arguments:
- layer_input: bfloat16 [8192, 8192], P('dp', 'col'), may hold values from -6 to 6
- query_cotangent: bfloat16 [8192, 4096], P('dp'), may hold values from -0.06591797 to 0.06591797
- key_cotangent: bfloat16 [8192, 1024], P('dp'), may hold values from -0.06591797 to 0.06591797
- up_cotangent: bfloat16 [8192, 14336], P('dp'), may hold values from -0.06591797 to 0.06591797
- query_weight: bfloat16 [4096, 8192], P('dp', 'col'), may hold values from -24 to 24
- key_weight: bfloat16 [1024, 8192], P('dp', 'col'), may hold values from -24 to 24
- up_weight: bfloat16 [14336, 8192], P('dp', 'col'), may hold values from -24 to 24
- moment_query: bfloat16 [4096, 8192], P('dp', 'col'), may hold values from -3 to 3
- moment_key: bfloat16 [1024, 8192], P('dp', 'col'), may hold values from -3 to 3
- moment_up: bfloat16 [14336, 8192], P('dp', 'col'), may hold values from -3 to 3
- second_query: bfloat16 [4096, 8192], P('dp', 'col'), may hold values from 0.25 to 4
- second_key: bfloat16 [1024, 8192], P('dp', 'col'), may hold values from 0.25 to 4
- second_up: bfloat16 [14336, 8192], P('dp', 'col'), may hold values from 0.25 to 4
Outputs:
- updated_query: bfloat16 [4096, 8192], P('dp', 'col')
- updated_key: bfloat16 [1024, 8192], P('dp', 'col')
- updated_up: bfloat16 [14336, 8192], P('dp', 'col')
- mean_query: bfloat16 [4096, 8192], P('dp', 'col')
- mean_key: bfloat16 [1024, 8192], P('dp', 'col')
- mean_up: bfloat16 [14336, 8192], P('dp', 'col')
- square_query: bfloat16 [4096, 8192], P('dp', 'col')
- square_key: bfloat16 [1024, 8192], P('dp', 'col')
- square_up: bfloat16 [14336, 8192], P('dp', 'col')
All inputs are finite; a program needn't handle non-finite values.
Results may differ from a plain program's by a relative error of at most 0.001.
Values may be sent and summed in bfloat16 or wider, within the bound.
A program may use at most 128 MiB of HBM per device.

v0:
```python
import jax
import jax.numpy as jnp
from jax import lax
from jax.sharding import PartitionSpec as P

beta_one = 0.9
beta_two = 0.95
rate = 0.1
eps_adam = 1e-08
eps_norm = 1e-06


def contract_tokens(cotangent_rows, inputs):
    return lax.dot_general(
        cotangent_rows, inputs, (((0,), (0,)), ((), ())), preferred_element_type=jnp.float32
    )


def optimizer_pass(gradient, weight, moment, second):
    first = beta_one * moment.astype(jnp.float32) + (1.0 - beta_one) * gradient
    square = beta_two * second.astype(jnp.float32) + (1.0 - beta_two) * gradient * gradient
    step = weight.astype(jnp.float32) - rate * first / (jnp.sqrt(square) + eps_adam)
    partial_power = jnp.sum(step * step, axis=1)
    return (step, first.astype(jnp.bfloat16), square.astype(jnp.bfloat16), partial_power)


def finish_rows(step, total_power, width):
    scale = jnp.sqrt(total_power / width + eps_norm)
    return (step / scale[:, None]).astype(jnp.bfloat16)


def per_device(
    layer_input,
    query_cotangent,
    key_cotangent,
    up_cotangent,
    query_weight,
    key_weight,
    up_weight,
    moment_query,
    moment_key,
    moment_up,
    second_query,
    second_key,
    second_up,
):
    groups = lax.axis_size("dp")
    tok_local = layer_input.shape[0]
    query_rows = query_weight.shape[0]
    key_rows = key_weight.shape[0]
    up_rows = up_weight.shape[0]
    all_rows = query_rows + key_rows + up_rows
    width = layer_input.shape[1] * lax.axis_size("col")
    joined = jnp.concatenate(
        [
            query_cotangent.reshape(tok_local, groups, query_rows),
            key_cotangent.reshape(tok_local, groups, key_rows),
            up_cotangent.reshape(tok_local, groups, up_rows),
        ],
        axis=2,
    )
    owned = lax.all_to_all(joined, "dp", split_axis=1, concat_axis=0, tiled=True).reshape(
        -1, all_rows
    )
    gathered = lax.all_gather(layer_input, "dp", axis=0, tiled=True)
    gradient = contract_tokens(owned, gathered)
    grad_query = gradient[:query_rows]
    grad_key = gradient[query_rows : query_rows + key_rows]
    grad_up = gradient[query_rows + key_rows :]
    step_query, first_query, sq_query, power_query = optimizer_pass(
        grad_query, query_weight, moment_query, second_query
    )
    step_key, first_key, sq_key, power_key = optimizer_pass(
        grad_key, key_weight, moment_key, second_key
    )
    step_up, first_up, sq_up, power_up = optimizer_pass(grad_up, up_weight, moment_up, second_up)
    total_query, total_key, total_up = lax.psum((power_query, power_key, power_up), "col")
    new_query = finish_rows(step_query, total_query, width)
    new_key = finish_rows(step_key, total_key, width)
    new_up = finish_rows(step_up, total_up, width)
    return (new_query, new_key, new_up, first_query, first_key, first_up, sq_query, sq_key, sq_up)


def solution(mesh):
    placed = (
        P("dp", "col"),
        P("dp", None),
        P("dp", None),
        P("dp", None),
        P("dp", "col"),
        P("dp", "col"),
        P("dp", "col"),
        P("dp", "col"),
        P("dp", "col"),
        P("dp", "col"),
        P("dp", "col"),
        P("dp", "col"),
        P("dp", "col"),
    )
    return jax.shard_map(
        per_device,
        mesh=mesh,
        in_specs=placed,
        out_specs=(
            P("dp", "col"),
            P("dp", "col"),
            P("dp", "col"),
            P("dp", "col"),
            P("dp", "col"),
            P("dp", "col"),
            P("dp", "col"),
            P("dp", "col"),
            P("dp", "col"),
        ),
        check_vma=False,
    )
```

profile of v0, /device:TPU:6, one launch (start us, length us, event | category | flops | bytes accessed | tf_op | source)
XLA Modules:
  0.0 440.0 jit_solution(7235209890121948709)
XLA Ops:
  7.2 0.0 all-gather.2.cloned.1.call-start
  7.2 0.7 all-gather.2.cloned.1.call-update
  7.9 6.1 %copy.24 = bf16[128,14336]{0,1:T(8,128)(2,1)} copy(bf16[128,14336]{1,0:T(8,128)(2,1)} %param.16) | data formatting | bytes 7340032 | tf_op args[3]
  14.1 0.7 copy.22
  14.7 0.2 copy.23
  14.9 2.2 pad_maximum_fusion
  17.2 182.4 %all_to_all.15 = bf16[128,64,304]{0,2,1:T(8,128)(2,1)S(1)} all-to-all(bf16[128,64,304]{0,2,1:T(8,128)(2,1)S(1)} %pad_maximum_fusion), channel_id=1, replica_groups=mesh['col'=4,'dp'=64] {'dp'}, dimensions={1} | all-to-all | bytes 9961472 | tf_op jit(solution)/shard_map/all_to_all | solution.py:62
  199.6 3.6 copy.25
  203.2 188.7 %all-gather.2.cloned.1.call-done = bf16[8192,2048]{1,0:T(8,128)(2,1)} async-done(((bf16[128,2048]{1,0:T(8,128)(2,1)}), bf16[8192,2048]{1,0:T(8,128)(2,1)}) %all-gather.2.cloned.1.call-update) | async-done | bytes 33554448 | tf_op jit(solution)/shard_map/all_gather | solution.py:65
  391.9 26.3 %fusion = f32[304,2048]{1,0:T(8,128)S(1)} fusion(bf16[8192,2048]{1,0:T(8,128)(2,1)} %all-gather.2.cloned.1.call-done, bf16[38,8,64,128]{3,2,1,0:T(8,128)(2,1)} %bitcast.16), kind=kOutput, calls=%fused_computation | convolution fusion | flops 10200547328 | bytes 41025536 | tf_op jit(solution)/shard_map/dot_general | solution.py:14
  418.3 0.0 copy-start.3
  418.3 0.0 copy-start.4
  418.3 0.0 copy-start.5
  418.3 0.0 copy-start.7
  418.3 0.0 copy-start.8
  418.3 0.0 copy-start.9
  418.3 4.2 multiply_reduce_fusion
  422.5 0.0 copy-done.4
  422.5 1.3 multiply_reduce_fusion.1
  423.9 0.9 multiply_reduce_fusion.2
  424.7 5.8 %all-reduce = (f32[64]{0:T(128)S(1)}, f32[16]{0:T(128)S(1)}, f32[224]{0:T(256)S(1)}) all-reduce(f32[64]{0:T(128)S(1)} %get-tuple-element.16, f32[16]{0:T(128)S(1)} %get-tuple-element.14, f32[224]{0:T(256)S(1)} %get-tuple-element.12), channel_id=1, replica_groups=mesh['col'=4,'dp'=64] {'col'}, use_global_device_ids=true, to_apply=%region_1.0 | all-reduce | flops 304 | bytes 2432 | tf_op jit(solution)/shard_map/psum | solution.py:77
  430.5 1.1 divide_convert_fusion
  431.7 0.7 divide_convert_fusion.2
  432.4 0.8 divide_convert_fusion.1
  (16 shorter events, 0.1 us)
Async XLA Ops:
  7.2 384.7 %all-gather.2.cloned.1.call-start = ((), (), s32[]{:S(2)}) async-start(), calls=%async_computation.1 | async-start | bytes 34078720 | tf_op jit(solution)/shard_map/all_gather | solution.py:65
  7.9 6.2 %copy-start = (bf16[128,4096]{1,0:T(8,128)(2,1)S(1)}, bf16[128,4096]{1,0:T(8,128)(2,1)}, u32[]{:S(2)}) copy-start(bf16[128,4096]{1,0:T(8,128)(2,1)} %param.14) | copy-start | bytes 3145732
  7.9 6.8 %copy-start.6 = (bf16[128,1024]{1,0:T(8,128)(2,1)S(1)}, bf16[128,1024]{1,0:T(8,128)(2,1)}, u32[]{:S(2)}) copy-start(bf16[128,1024]{1,0:T(8,128)(2,1)} %param.15) | copy-start | bytes 786436
  391.9 26.3 %copy-start.1 = (bf16[224,2048]{1,0:T(8,128)(2,1)S(1)}, bf16[224,2048]{1,0:T(8,128)(2,1)}, u32[]{:S(2)}) copy-start(bf16[224,2048]{1,0:T(8,128)(2,1)} %param.25) | copy-start | bytes 2752516
  391.9 26.3 %copy-start.2 = (bf16[224,2048]{1,0:T(8,128)(2,1)S(1)}, bf16[224,2048]{1,0:T(8,128)(2,1)}, u32[]{:S(2)}) copy-start(bf16[224,2048]{1,0:T(8,128)(2,1)} %param.22) | copy-start | bytes 2752516
  418.3 4.2 copy-start.3
  418.3 4.2 copy-start.4
  418.3 4.2 copy-start.5
  418.3 5.5 %copy-start.7 = (bf16[16,2048]{1,0:T(8,128)(2,1)S(1)}, bf16[16,2048]{1,0:T(8,128)(2,1)}, u32[]{:S(2)}) copy-start(bf16[16,2048]{1,0:T(8,128)(2,1)} %param.24) | copy-start | bytes 196612
  418.3 5.5 %copy-start.8 = (bf16[16,2048]{1,0:T(8,128)(2,1)S(1)}, bf16[16,2048]{1,0:T(8,128)(2,1)}, u32[]{:S(2)}) copy-start(bf16[16,2048]{1,0:T(8,128)(2,1)} %param.21) | copy-start | bytes 196612
  418.3 5.5 %copy-start.9 = (bf16[16,2048]{1,0:T(8,128)(2,1)S(1)}, bf16[16,2048]{1,0:T(8,128)(2,1)}, u32[]{:S(2)}) copy-start(bf16[16,2048]{1,0:T(8,128)(2,1)} %param.18) | copy-start | bytes 196612
Sparse Core Ops, SparseCore 0:
  11.3 380.5 all-gather.1
where the time goes:
time: 440 us
  waiting for transfers between devices  189 us (43%)
  blocking collectives  188 us (43%)
  matrix products  26.3 us (6%)
  between operations  14.2 us (3%)
  other arithmetic  11.3 us (3%)
  local copies, waits for them, and re-layouts  10.7 us (2%)
    all_gather x1, waiting for transfers between devices, per_device(): gathered = lax.all_gather(layer_input, 'dp', axis=0, tiled=True)  189 us
    all_to_all x1, blocking collectives, per_device(): lax.all_to_all(joined, 'dp', split_axis=1, concat_axis=0, tiled=True)  182 us
    dot_general x1, matrix products, contract_tokens(): lax.dot_general(cotangent_rows, inputs, (((0,), (0,)), ((), ())), preferr...  26.3 us
  transfers between devices with their start and end apart: 1, of which 1 were waited for; matrix products, arithmetic and copies ran while one was open for 3% of the time, Pallas kernels for 0%

commit v1 on v0

--- a/solution.py
+++ b/solution.py
@@ -62,7 +62,9 @@
     owned = lax.all_to_all(joined, "dp", split_axis=1, concat_axis=0, tiled=True).reshape(
         -1, all_rows
     )
-    gathered = lax.all_gather(layer_input, "dp", axis=0, tiled=True)
+    gathered = jnp.concatenate(
+        lax.all_to_all(jnp.stack([layer_input] * lax.axis_size("dp")), "dp", 0, 0), axis=0
+    )
     gradient = contract_tokens(owned, gathered)
     grad_query = gradient[:query_rows]
     grad_key = gradient[query_rows : query_rows + key_rows]

time: 440 us -> 1030 us (2.34)
  the two profiles are of different devices: /device:TPU:6 before, /device:TPU:162 now
where the time goes in v1:
time: 1030 us
  waiting for transfers between devices  823 us (80%)
  blocking collectives  129 us (13%)
  matrix products  26.2 us (3%)
  local copies, waits for them, and re-layouts  23.9 us (2%)
  other arithmetic  11.6 us (1%)
  starting transfers between devices  11.3 us (1%)
    all_to_all x1, waiting for transfers between devices, per_device(): lax.all_to_all(jnp.stack([layer_input] * lax.axis_size('dp')), 'dp', 0, 0)  823 us
    all_to_all x1, blocking collectives, per_device(): lax.all_to_all(joined, 'dp', split_axis=1, concat_axis=0, tiled=True)  123 us
    dot_general x1, matrix products, contract_tokens(): lax.dot_general(cotangent_rows, inputs, (((0,), (0,)), ((), ())), preferr...  26.2 us
  transfers between devices with their start and end apart: 1, of which 1 were waited for; matrix products, arithmetic and copies ran while one was open for 1% of the time, Pallas kernels for 0%

profile of v1, /device:TPU:162, one launch (start us, length us, event | category | flops | bytes accessed | tf_op | source)
XLA Modules:
  0.0 1025.9 jit_solution(17596896096685570473)
XLA Ops:
  0.7 6.1 copy.24
  6.8 0.7 copy.22
  7.5 0.2 copy.23
  7.6 2.2 pad_maximum_fusion
  9.9 0.0 copy-start.2
  9.9 123.2 %all_to_all.20 = bf16[128,64,304]{0,2,1:T(8,128)(2,1)} all-to-all(bf16[128,64,304]{0,2,1:T(8,128)(2,1)S(1)} %pad_maximum_fusion), channel_id=1, replica_groups=mesh['col'=4,'dp'=64] {'dp'}, dimensions={1} | all-to-all | bytes 9961472 | tf_op jit(solution)/shard_map/all_to_all | solution.py:62
  133.1 11.0 %stack.2 = bf16[64,128,2048]{2,1,0:T(8,128)(2,1)} broadcast(bf16[128,2048]{1,0:T(8,128)(2,1)S(1)} %copy-done.2), dimensions={1,2} | broadcast | bytes 34078720 | tf_op jit(solution)/shard_map/stack | solution.py:66
  144.1 11.3 %all-to-all-start.1 = ((bf16[64,128,2048]{2,1,0:T(8,128)(2,1)}), bf16[64,128,2048]{2,1,0:T(8,128)(2,1)}, u32[]{:S(2)}, u32[]{:S(2)}) async-start(bf16[64,128,2048]{2,1,0:T(8,128)(2,1)} %stack.2), calls=%async_computation.1 | async-start | bytes 67108864 | tf_op jit(solution)/shard_map/all_to_all | solution.py:66
  155.4 6.0 copy.25
  161.3 823.1 %all-to-all-done.1 = bf16[64,128,2048]{2,1,0:T(8,128)(2,1)} async-done(((bf16[64,128,2048]{2,1,0:T(8,128)(2,1)}), bf16[64,128,2048]{2,1,0:T(8,128)(2,1)}, u32[]{:S(2)}, u32[]{:S(2)}) %all-to-all-start.1) | async-done | bytes 33554464 | tf_op jit(solution)/shard_map/all_to_all | solution.py:66
  984.4 26.2 %fusion = f32[304,2048]{1,0:T(8,128)S(1)} fusion(bf16[8192,2048]{1,0:T(8,128)(2,1)} %bitcast.5, bf16[38,8,64,128]{3,2,1,0:T(8,128)(2,1)} %bitcast.17), kind=kOutput, calls=%fused_computation | convolution fusion | flops 10200547328 | bytes 41025536 | tf_op jit(solution)/shard_map/dot_general | solution.py:14
  1010.7 0.0 copy-start.3
  1010.7 0.0 copy-start.4
  1010.7 0.0 copy-start.5
  1010.7 0.0 copy-start.7
  1010.7 0.0 copy-start.8
  1010.7 0.0 copy-start.9
  1010.8 4.5 multiply_reduce_fusion
  1015.2 1.3 multiply_reduce_fusion.1
  1016.6 0.9 multiply_reduce_fusion.2
  1017.4 5.8 all-reduce
  1023.2 1.1 divide_convert_fusion
  1024.4 0.7 divide_convert_fusion.2
  1025.1 0.8 divide_convert_fusion.1
  (16 shorter events, 0.1 us)
Async XLA Ops:
  0.6 6.2 copy-start
  0.7 6.8 copy-start.6
  9.9 123.2 %copy-start.2 = (bf16[128,2048]{1,0:T(8,128)(2,1)S(1)}, bf16[128,2048]{1,0:T(8,128)(2,1)}, u32[]{:S(2)}) copy-start(bf16[128,2048]{1,0:T(8,128)(2,1)} %param.13) | copy-start | bytes 1572868
  144.1 840.3 %all-to-all-start.1 = ((bf16[64,128,2048]{2,1,0:T(8,128)(2,1)}), bf16[64,128,2048]{2,1,0:T(8,128)(2,1)}, u32[]{:S(2)}, u32[]{:S(2)}) async-start(bf16[64,128,2048]{2,1,0:T(8,128)(2,1)} %stack.2), calls=%async_computation.1 | async-start | bytes 67108864 | tf_op jit(solution)/shard_map/all_to_all | solution.py:66
  984.4 26.3 %copy-start.1 = (bf16[224,2048]{1,0:T(8,128)(2,1)S(1)}, bf16[224,2048]{1,0:T(8,128)(2,1)}, u32[]{:S(2)}) copy-start(bf16[224,2048]{1,0:T(8,128)(2,1)} %param.25) | copy-start | bytes 2752516
  1010.7 4.5 copy-start.3
  1010.7 4.5 copy-start.4
  1010.7 4.5 copy-start.5
  1010.7 5.8 copy-start.7
  1010.7 5.8 copy-start.8
  1010.7 5.8 copy-start.9
